TPU v7x, 32 devices: a whole 2x2x4 slice. The times are simulated.
32 devices in a mesh: groups: 2 (over y), blk: 4 (over z), head: 2 (over x), pair: 2 (over core).
Axes of the slice: x: 2, y: 2, z: 4, core: 2. Of those that a mesh axis runs over, the one named last changes fastest.
Arguments:
- single: bfloat16 [256, 384], P(('groups', 'blk')), parts along dimension 0, may hold values from -6 to 6
- pair: bfloat16 [256, 4, 32, 128], P(('groups', 'blk'), None, 'pair'), parts along dimension 0, may hold values from -6 to 6
- frames: float32 [12, 256], P(None, ('groups', 'blk')), parts along dimension 1, as said below
- chain: int32 [256], P(('groups', 'blk')), parts along dimension 0, may hold values from 0 to 5, never falling along the last dimension, each value on 1 to 42 neighbouring positions
- mask: int32 [256], P(('groups', 'blk')), parts along dimension 0, may hold values 0 or 1
- w_query: bfloat16 [384, 192], P(None, 'head'), may hold values from -0.3125 to 0.3125
- w_key_value: bfloat16 [384, 384], P(None, 'head'), may hold values from -0.3125 to 0.3125
- w_query_points: bfloat16 [384, 144], P(None, 'head'), may hold values from -0.3125 to 0.3125
- w_kv_points: bfloat16 [384, 432], P(None, 'head'), may hold values from -0.3125 to 0.3125
- w_pair_bias: bfloat16 [128, 12], P(None, 'head'), may hold values from -0.5 to 0.5
- head_weights: float32 [12], P('head'), may hold values from -9 to 1
- chain_bias: float32 [12], P('head'), may hold values from -3 to 3
- w_out: bfloat16 [12, 176, 384], P('head'), may hold values from -0.125 to 0.125
- out_gain: float32 [384], replicated, may hold values from 0.5 to 1.5
- w_backbone: bfloat16 [384, 6], replicated, may hold values from -0.3125 to 0.3125
Outputs:
- single_out: bfloat16 [256, 384], P(('groups', 'blk')), parts along dimension 0
- frames_out: float32 [12, 256], P(None, 'groups'), parts along dimension 1
There are 2 independent parts, one for each index of `groups`. A program takes and returns all parts, laid end to end along the dimension named above; an argument that names none is the same for every part. Nothing has to cross between parts.
Inputs may be any that keep to these rules, and one draw needn't show every extreme that they name: `frames`: rows 0 to 8 of every column hold an orthonormal rotation matrix row by row; rows 9 to 11 the translation.
All inputs are finite; a program needn't handle non-finite values. No bound on the sum of `mask` on one device may be relied on, other than what follows from the above.
Results may differ from a plain program's by a relative error of at most 0.0048.
Values sent between devices are 32-bit elements; how exact they have to be, the bound alone decides.
A program may use at most 64 MiB of HBM per device.

v0:
```python
import math
import jax
import jax.numpy as jnp
from jax import lax
from jax.sharding import PartitionSpec as P

HIGH = lax.Precision.HIGHEST
LOGIT_WEIGHT = math.sqrt(1.0 / 3.0)
MASK_PENALTY = 100000.0


def shifted(array, axis, by):
    peers = lax.axis_size(axis)
    return lax.ppermute(array, axis, [(i, (i + by) % peers) for i in range(peers)])


def combined_all(value, axis, join):
    pieces = jax.tree.map(lambda part: lax.all_gather(part, axis), value)
    head = jax.tree.map(lambda part: part[0], pieces)
    tail = jax.tree.map(lambda part: part[1:], pieces)
    so_far, _ = lax.scan(lambda so_far, section: (join(so_far, section), None), head, tail)
    return so_far


def to_global(local, frames):
    rotation = frames[:9].reshape(3, 3, -1)
    moved = jnp.einsum("abn,ngb->nga", rotation, local, precision=HIGH)
    return moved + jnp.transpose(frames[9:12])[:, None, :]


def to_local(points, frames):
    rotation = frames[:9].reshape(3, 3, -1)
    moved = points - jnp.transpose(frames[9:12])[:, None, None, :]
    return jnp.einsum("abn,nhpa->nhpb", rotation, moved, precision=HIGH)


def compose(frames, motion):
    rotation = frames[:9].reshape(3, 3, -1)
    inverse = 1.0 / jnp.sqrt(1.0 + motion[:, 0] ** 2 + motion[:, 1] ** 2 + motion[:, 2] ** 2)
    quat_b = motion[:, 0] * inverse
    quat_c = motion[:, 1] * inverse
    quat_d = motion[:, 2] * inverse
    spin = jnp.stack(
        [
            inverse * inverse + quat_b * quat_b - quat_c * quat_c - quat_d * quat_d,
            2.0 * (quat_b * quat_c - inverse * quat_d),
            2.0 * (quat_b * quat_d + inverse * quat_c),
            2.0 * (quat_b * quat_c + inverse * quat_d),
            inverse * inverse - quat_b * quat_b + quat_c * quat_c - quat_d * quat_d,
            2.0 * (quat_c * quat_d - inverse * quat_b),
            2.0 * (quat_b * quat_d - inverse * quat_c),
            2.0 * (quat_c * quat_d + inverse * quat_b),
            inverse * inverse - quat_b * quat_b - quat_c * quat_c + quat_d * quat_d,
        ]
    ).reshape(3, 3, -1)
    new_rotation = jnp.einsum("abn,bcn->acn", rotation, spin, precision=HIGH)
    offset = jnp.einsum("abn,nb->an", rotation, motion[:, 3:6], precision=HIGH)
    return jnp.concatenate([new_rotation.reshape(9, -1), frames[9:12] + offset], axis=0)


def attention_logits(
    pair_rows,
    query_rows,
    query_points,
    query_chain,
    query_present,
    keys,
    key_points,
    key_chain,
    key_present,
    w_pair_bias,
    distance_scale,
    chain_bias,
):
    count_q = pair_rows.shape[0]
    count_k = pair_rows.shape[1]
    bias = jnp.dot(
        pair_rows.reshape(count_q * count_k, -1), w_pair_bias, preferred_element_type=jnp.float32
    ).reshape(count_q, count_k, -1)
    dots = jnp.einsum("ihc,jhc->ijh", query_rows, keys, precision=HIGH) / math.sqrt(keys.shape[-1])
    gaps = query_points[:, None] - key_points[None]
    distance = jnp.sum(gaps * gaps, axis=(3, 4))
    differ = (query_chain[:, None] != key_chain[None, :]).astype(jnp.float32)
    logits = LOGIT_WEIGHT * (
        dots + bias - distance_scale * distance + chain_bias * differ[..., None]
    )
    absent = 1.0 - query_present[:, None] * key_present[None, :]
    return logits - MASK_PENALTY * absent[..., None]


def rescale(values, factor):
    return values * factor.reshape(factor.shape + (1,) * (values.ndim - factor.ndim))


def fold_pair(first, second):
    best = jnp.maximum(first[0], second[0])
    first_scale = jnp.exp(first[0] - best)
    second_scale = jnp.exp(second[0] - best)
    merged = [
        rescale(left_part, first_scale) + rescale(right_part, second_scale)
        for left_part, right_part in zip(first[1:], second[1:])
    ]
    return (best,) + tuple(merged)


def body(
    single,
    pair,
    frames,
    chain,
    mask,
    w_query,
    w_key_value,
    w_query_points,
    w_kv_points,
    w_pair_bias,
    head_weights,
    chain_bias,
    w_out,
    out_gain,
    w_backbone,
):
    rows = single.shape[0]
    half = pair.shape[2]
    width = pair.shape[3]
    heads_here = w_pair_bias.shape[1]
    head_size = w_query.shape[1] // heads_here
    query_count = w_query_points.shape[1] // (3 * heads_here)
    value_count = w_kv_points.shape[1] // (3 * heads_here) - query_count
    pair_keys = pair.reshape(rows, pair.shape[1] * half, width)
    query = jnp.dot(single, w_query, preferred_element_type=jnp.float32).reshape(
        rows, heads_here, head_size
    )
    query_local = jnp.dot(single, w_query_points, preferred_element_type=jnp.float32)
    query_points = to_global(query_local.reshape(rows, heads_here * query_count, 3), frames)
    query_points = query_points.reshape(rows, heads_here, query_count, 3)
    query_chain = chain.astype(jnp.float32)
    query_present = mask.astype(jnp.float32)
    distance_scale = jax.nn.softplus(head_weights) * math.sqrt(2.0 / (9.0 * query_count)) / 2.0
    position = lax.axis_index("pair")
    key_single = lax.dynamic_slice_in_dim(single, position * half, half, 0)
    key_frames = lax.dynamic_slice_in_dim(frames, position * half, half, 1)
    key_chain = lax.dynamic_slice_in_dim(query_chain, position * half, half, 0)
    key_present = lax.dynamic_slice_in_dim(query_present, position * half, half, 0)
    key_value = jnp.dot(key_single, w_key_value, preferred_element_type=jnp.float32)
    key_local = jnp.dot(key_single, w_kv_points, preferred_element_type=jnp.float32)
    key_global = to_global(
        key_local.reshape(half, heads_here * (query_count + value_count), 3), key_frames
    )
    payload = jnp.concatenate([key_value, key_global.reshape(half, -1)], axis=1)
    key_meta = jnp.stack([key_chain, key_present], axis=1)
    split_at = heads_here * 2 * head_size

    def absorb(carry, moving, moving_meta, start):
        top, total, sum_values, sum_points, sum_pair = carry
        count = moving.shape[0]
        pieces = moving[:, :split_at].reshape(count, heads_here, 2, head_size)
        points = moving[:, split_at:].reshape(count, heads_here, query_count + value_count, 3)
        pair_rows = lax.dynamic_slice_in_dim(pair_keys, start, count, 1)
        logits = attention_logits(
            pair_rows,
            query,
            query_points,
            query_chain,
            query_present,
            pieces[:, :, 0],
            points[:, :, :query_count],
            moving_meta[:, 0],
            moving_meta[:, 1],
            w_pair_bias,
            distance_scale,
            chain_bias,
        )
        new_top = jnp.maximum(top, jnp.max(logits, axis=1))
        scale = jnp.exp(top - new_top)
        weights = jnp.exp(logits - new_top[:, None, :])
        total = total * scale + jnp.sum(weights, axis=1)
        sum_values = sum_values * scale[..., None] + jnp.einsum(
            "ijh,jhc->ihc", weights, pieces[:, :, 1], precision=HIGH
        )
        sum_points = sum_points * scale[..., None, None] + jnp.einsum(
            "ijh,jhpd->ihpd", weights, points[:, :, query_count:], precision=HIGH
        )
        sum_pair = sum_pair * scale[..., None] + jnp.einsum(
            "ijh,ijc->ihc",
            weights.astype(jnp.bfloat16),
            pair_rows,
            preferred_element_type=jnp.float32,
        )
        return (new_top, total, sum_values, sum_points, sum_pair)

    initial = (
        jnp.full((rows, heads_here), -1e30, jnp.float32),
        jnp.zeros((rows, heads_here), jnp.float32),
        jnp.zeros((rows, heads_here, head_size), jnp.float32),
        jnp.zeros((rows, heads_here, value_count, 3), jnp.float32),
        jnp.zeros((rows, heads_here, width), jnp.float32),
    )
    block = lax.axis_index("blk")
    blocks = lax.axis_size("blk")
    carry = absorb(initial, payload, key_meta, block * half)

    def advance(step, state):
        carry, moving, moving_meta = state
        moving, moving_meta = shifted((moving, moving_meta), "blk", 1)
        source = (block - step) % blocks
        return (absorb(carry, moving, moving_meta, source * half), moving, moving_meta)

    carry = lax.fori_loop(1, blocks, advance, (carry, payload, key_meta))[0]
    best, total, sum_values, sum_points, sum_pair = combined_all(carry, "pair", fold_pair)
    attended = sum_values / total[..., None]
    pointed = to_local(sum_points / total[..., None, None], frames)
    point_norms = jnp.sqrt(jnp.sum(pointed * pointed, axis=3) + 1.0)
    paired = sum_pair / total[..., None]
    joined = jnp.concatenate(
        [attended, pointed.reshape(rows, heads_here, value_count * 3), point_norms, paired], axis=2
    ).astype(jnp.bfloat16)
    partial_update = jnp.dot(
        joined.reshape(rows, -1),
        w_out.reshape(-1, w_out.shape[2]),
        preferred_element_type=jnp.float32,
    )
    update = lax.psum(partial_update, "head")
    mixed = single.astype(jnp.float32) + update
    centre = jnp.mean(mixed, axis=1, keepdims=True)
    spread = jnp.mean(jnp.square(mixed - centre), axis=1, keepdims=True)
    single_out = ((mixed - centre) * lax.rsqrt(spread + 1e-05) * out_gain).astype(jnp.bfloat16)
    motion = jnp.dot(single_out, w_backbone, preferred_element_type=jnp.float32)
    frames_new = compose(frames, motion)
    frames_out = lax.all_gather(frames_new, "blk", axis=1, tiled=True)
    return (single_out, frames_out)


def solution(mesh):
    placed = (
        P(("groups", "blk"), None),
        P(("groups", "blk"), None, "pair", None),
        P(None, ("groups", "blk")),
        P(("groups", "blk")),
        P(("groups", "blk")),
        P(None, "head"),
        P(None, "head"),
        P(None, "head"),
        P(None, "head"),
        P(None, "head"),
        P("head"),
        P("head"),
        P("head", None, None),
        P(),
        P(),
    )
    return jax.shard_map(
        body,
        mesh=mesh,
        in_specs=placed,
        out_specs=(P(("groups", "blk"), None), P(None, "groups")),
        check_vma=False,
    )
```

profile of v0, /device:TPU:0, one launch (start us, length us, event | category | flops | bytes accessed | tf_op | source)
XLA Modules:
  0.0 85.5 jit_solution(7720689807309747148)
XLA Ops:
  0.7 0.7 copy-done.13
  1.7 0.3 copy-done.8
  2.6 0.6 copy-done.3
  3.1 1.1 %fusion.59 = f32[16,192]{1,0:T(8,128)S(1)} fusion(bf16[384,192]{0,1:T(8,128)(2,1)} %param.23, bf16[32,384]{1,0:T(8,128)(2,1)S(1)} %copy-done.3, s32[]{:T(128)S(6)} %select_n.43), kind=kOutput, calls=%fused_computation.96 | convolution fusion | flops 2359296 | bytes 172036 | tf_op jit(solution)/shard_map/dot_general | solution.py:145
  4.6 0.8 copy-done.7
  5.7 0.3 convolution_add_fusion.2
  6.6 0.7 copy-done.4
  7.7 0.3 convolution_add_fusion.3
  8.4 0.3 copy-done.2
  8.7 0.3 copy-done.6
  9.0 0.4 fusion.35
  9.6 0.2 copy.240
  9.8 0.2 multiply_reduce_fusion.1
  10.1 0.4 copy-done.10
  10.5 0.2 fusion.84
  11.6 0.4 fusion.20
  12.0 35.5 %while.7 = (s32[]{:T(128)}, f32[32,6]{0,1:T(8,128)S(1)}, f32[32,6]{0,1:T(8,128)S(1)}, f32[32,6,16]{0,2,1:T(8,128)S(1)}, f32[32,6,8,3]{0,2,3,1:T(8,128)S(1)}, /*i...) while((s32[]{:T(128)}, f32[32,6]{0,1:T(8,128)S(1)}, ...), condition=%wide.region_7.8_spmd, body=%wide.region_3.7_spmd.sunk | while | flops 3855250 | bytes 1648512 | solution.py:209
  12.0 3.1 %collective-permute-start = (f32[16,2]{0,1:T(2,128)S(1)}, f32[16,2]{0,1:T(2,128)S(1)}, u32[]{:S(2)}, u32[]{:S(2)}) collective-permute-start(f32[16,2]{0,1:T(2,128)S(1)} %get-tuple-element.757), channel_id=1, source_target_pairs={{0,4},{4,8},{8,12},{12,0},{1,5},{5,9},{9,13},{13,1},{2,6},{6,10},{... | collective-permute-start | bytes 392 | tf_op jit(solution)/shard_map/while/body/eval_jaxpr/ppermute | solution.py:14
  15.1 1.6 %collective-permute-start.1 = (f32[16,408]{0,1:T(8,128)S(1)}, f32[16,408]{0,1:T(8,128)S(1)}, u32[]{:S(2)}, u32[]{:S(2)}) collective-permute-start(f32[16,408]{0,1:T(8,128)S(1)} %get-tuple-element.756), channel_id=1, source_target_pairs={{0,4},{4,8},{8,12},{12,0},{1,5},{5,9},{9,13},{13,1},{2,6},{6,10},{... | collective-permute-start | bytes 78344 | tf_op jit(solution)/shard_map/while/body/eval_jaxpr/ppermute | solution.py:14
  16.7 0.4 fusion.127
  17.2 1.5 %collective-permute-done = f32[16,2]{0,1:T(2,128)S(1)} collective-permute-done((f32[16,2]{0,1:T(2,128)S(1)}, f32[16,2]{0,1:T(2,128)S(1)}, u32[]{:S(2)}, u32[]{:S(2)}) %collective-permute-start) | collective-permute-done | bytes 160 | tf_op jit(solution)/shard_map/while/body/eval_jaxpr/ppermute | solution.py:14
  18.9 4.7 %collective-permute-done.1 = f32[16,408]{0,1:T(8,128)S(1)} collective-permute-done((f32[16,408]{0,1:T(8,128)S(1)}, f32[16,408]{0,1:T(8,128)S(1)}, u32[]{:S(2)}, u32[]{:S(2)}) %collective-permute-start.1) | collective-permute-done | bytes 26144 | tf_op jit(solution)/shard_map/while/body/eval_jaxpr/ppermute | solution.py:14
  23.7 0.6 copy-done.1
  24.3 0.2 multiply_reduce_fusion.6
  24.5 0.3 fusion.128
  25.3 0.6 slice-done
  25.9 0.3 fusion.131
  26.2 0.2 convolution_add_fusion.5
  26.5 1.4 %collective-permute-start.1 = (f32[16,408]{0,1:T(8,128)S(1)}, f32[16,408]{0,1:T(8,128)S(1)}, u32[]{:S(2)}, u32[]{:S(2)}) collective-permute-start(f32[16,408]{0,1:T(8,128)S(1)} %get-tuple-element.756), channel_id=1, source_target_pairs={{0,4},{4,8},{8,12},{12,0},{1,5},{5,9},{9,13},{13,1},{2,6},{6,10},{... | collective-permute-start | bytes 78344 | tf_op jit(solution)/shard_map/while/body/eval_jaxpr/ppermute | solution.py:14
  27.8 0.4 fusion.127
  28.3 3.5 %collective-permute-done = f32[16,2]{0,1:T(2,128)S(1)} collective-permute-done((f32[16,2]{0,1:T(2,128)S(1)}, f32[16,2]{0,1:T(2,128)S(1)}, u32[]{:S(2)}, u32[]{:S(2)}) %collective-permute-start) | collective-permute-done | bytes 160 | tf_op jit(solution)/shard_map/while/body/eval_jaxpr/ppermute | solution.py:14
  32.0 2.1 %collective-permute-done.1 = f32[16,408]{0,1:T(8,128)S(1)} collective-permute-done((f32[16,408]{0,1:T(8,128)S(1)}, f32[16,408]{0,1:T(8,128)S(1)}, u32[]{:S(2)}, u32[]{:S(2)}) %collective-permute-start.1) | collective-permute-done | bytes 26144 | tf_op jit(solution)/shard_map/while/body/eval_jaxpr/ppermute | solution.py:14
  34.2 0.6 copy-done.1
  34.9 0.2 multiply_reduce_fusion.6
  35.1 0.3 fusion.128
  35.9 0.6 slice-done
  36.4 0.3 fusion.131
  36.7 0.2 convolution_add_fusion.5
  37.1 0.6 collective-permute-start.1
  37.7 0.4 fusion.127
  38.2 4.3 %collective-permute-done = f32[16,2]{0,1:T(2,128)S(1)} collective-permute-done((f32[16,2]{0,1:T(2,128)S(1)}, f32[16,2]{0,1:T(2,128)S(1)}, u32[]{:S(2)}, u32[]{:S(2)}) %collective-permute-start) | collective-permute-done | bytes 160 | tf_op jit(solution)/shard_map/while/body/eval_jaxpr/ppermute | solution.py:14
  42.6 2.1 %collective-permute-done.1 = f32[16,408]{0,1:T(8,128)S(1)} collective-permute-done((f32[16,408]{0,1:T(8,128)S(1)}, f32[16,408]{0,1:T(8,128)S(1)}, u32[]{:S(2)}, u32[]{:S(2)}) %collective-permute-start.1) | collective-permute-done | bytes 26144 | tf_op jit(solution)/shard_map/while/body/eval_jaxpr/ppermute | solution.py:14
  44.8 0.6 copy-done.1
  45.4 0.2 multiply_reduce_fusion.6
  45.7 0.3 fusion.128
  46.4 0.6 slice-done
  47.0 0.3 fusion.131
  47.3 0.2 convolution_add_fusion.5
  47.6 1.8 %all-gather.5 = f32[2,32,6]{1,2,0:T(8,128)S(1)} all-gather(f32[1,32,6]{1,2,0:T(8,128)S(1)} %bitcast.281), channel_id=3, replica_groups=mesh['groups'=2,'blk'=4,'head'=2,'pair'=2] {'pair'}, dimensions={0}, use_global_device_ids=true | all-gather | bytes 2304 | tf_op jit(solution)/shard_map/all_gather | solution.py:18
  49.4 1.8 %all-gather.6 = f32[2,32,6]{1,2,0:T(8,128)S(1)} all-gather(f32[1,32,6]{1,2,0:T(8,128)S(1)} %bitcast.282), channel_id=4, replica_groups=mesh['groups'=2,'blk'=4,'head'=2,'pair'=2] {'pair'}, dimensions={0}, use_global_device_ids=true | all-gather | bytes 2304 | tf_op jit(solution)/shard_map/all_gather | solution.py:18
  51.5 1.9 %all-gather.4 = f32[64,6,128]{2,0,1:T(8,128)S(1)} all-gather(f32[32,6,128]{2,0,1:T(8,128)S(1)} %copy.259), channel_id=6, replica_groups=mesh['groups'=2,'blk'=4,'head'=2,'pair'=2] {'pair'}, dimensions={0}, use_global_device_ids=true | all-gather | bytes 294912 | tf_op jit(solution)/shard_map/all_gather | solution.py:18
  53.7 1.9 %all-gather = f32[64,6,16]{2,0,1:T(8,128)S(1)} all-gather(f32[32,6,16]{2,0,1:T(8,128)S(1)} %copy.249), channel_id=2, replica_groups=mesh['groups'=2,'blk'=4,'head'=2,'pair'=2] {'pair'}, dimensions={0}, use_global_device_ids=true | all-gather | bytes 36864 | tf_op jit(solution)/shard_map/all_gather | solution.py:18
  55.8 0.2 copy.250
  56.0 2.4 %all-gather.3 = f32[64,6,8,3]{2,1,3,0:T(8,128)S(1)} all-gather(f32[32,6,8,3]{2,1,3,0:T(8,128)S(1)} %copy.250), channel_id=5, replica_groups=mesh['groups'=2,'blk'=4,'head'=2,'pair'=2] {'pair'}, dimensions={0}, use_global_device_ids=true | all-gather | bytes 55296 | tf_op jit(solution)/shard_map/all_gather | solution.py:18
  58.4 0.3 fusion.30
  58.6 1.1 %fusion.82 = (bf16[32,6,8,3]{2,3,1,0:T(4,128)(2,1)S(1)}, f32[32,6,8]{2,1,0:T(8,128)S(1)}) fusion(f32[3,3,32,1]{0,1,3,2:T(4,128)S(1)} %copy.271, f32[32,6,8,3]{2,1,3,0:T(8,128)S(1)} %fusion.30), kind=kOutput, calls=%fused_computation.152 | convolution fusion | flops 178176 | bytes 34944 | tf_op jit(solution)/shard_map/abn,nhpa->nhpb/dot_general | solution.py:34
  59.7 0.2 copy.257
  60.3 0.4 convolution_bitcast_fusion.4
  60.7 8.6 %psum.7 = f32[32,384]{1,0:T(8,128)S(1)} all-reduce(f32[32,384]{1,0:T(8,128)S(1)} %convolution_bitcast_fusion.4), channel_id=1, replica_groups=mesh['groups'=2,'blk'=4,'head'=2,'pair'=2] {'head'}, use_global_device_ids=true, to_apply=%region_9.10 | all-reduce | flops 12288 | bytes 98304 | tf_op jit(solution)/shard_map/psum | solution.py:223
  69.7 0.6 copy-done.11
  70.5 0.4 copy-done.5
  71.1 0.3 convolution_bitcast_fusion.3
  71.6 13.1 %all-gather.7 = f32[4,32,12]{1,2,0:T(8,128)S(1)} all-gather(f32[1,32,12]{1,2,0:T(8,128)S(1)} %maximum_bitcast_fusion), channel_id=1, replica_groups=mesh['groups'=2,'blk'=4,'head'=2,'pair'=2] {'blk'}, dimensions={0}, use_global_device_ids=true | all-gather | bytes 7680 | tf_op jit(solution)/shard_map/all_gather | solution.py:230
  84.8 0.7 reshape.714
  (160 shorter events, 8.1 us)
Async XLA Ops:
  0.6 59.6 %copy-start = (bf16[6,176,384]{2,1,0:T(8,128)(2,1)S(1)}, bf16[6,176,384]{2,1,0:T(8,128)(2,1)}, u32[]{:S(2)}) copy-start(bf16[6,176,384]{2,1,0:T(8,128)(2,1)} %param.29) | copy-start | bytes 2433028
  0.7 0.7 copy-start.13
  0.7 0.7 copy-start.14
  0.7 0.7 copy-start.15
  1.4 0.7 copy-start.8
  2.4 0.7 copy-start.3
  3.1 1.2 %copy-start.9 = (bf16[384,72]{0,1:T(8,128)(2,1)S(1)}, bf16[384,72]{0,1:T(8,128)(2,1)}, u32[]{:S(2)}) copy-start(bf16[384,72]{0,1:T(8,128)(2,1)} %param.24) | copy-start | bytes 165892
  4.5 0.9 %copy-start.7 = (bf16[384,96]{0,1:T(8,128)(2,1)S(1)}, bf16[384,96]{0,1:T(8,128)(2,1)}, u32[]{:S(2)}) copy-start(bf16[384,96]{0,1:T(8,128)(2,1)} %param.22) | copy-start | bytes 221188
  6.5 0.9 %copy-start.4 = (bf16[384,216]{0,1:T(8,128)(2,1)S(1)}, bf16[384,216]{0,1:T(8,128)(2,1)}, u32[]{:S(2)}) copy-start(bf16[384,216]{0,1:T(8,128)(2,1)} %param.25) | copy-start | bytes 497668
  7.6 1.0 %copy-start.2 = (bf16[32,4,16,128]{3,2,1,0:T(8,128)(2,1)S(1)}, bf16[32,4,16,128]{3,2,1,0:T(8,128)(2,1)}, u32[]{:S(2)}) copy-start(bf16[32,4,16,128]{3,2,1,0:T(8,128)(2,1)} %param.18) | copy-start | bytes 1572868
  8.3 0.7 copy-start.6
  9.8 0.7 copy-start.10
  12.0 6.7 %collective-permute-start = (f32[16,2]{0,1:T(2,128)S(1)}, f32[16,2]{0,1:T(2,128)S(1)}, u32[]{:S(2)}, u32[]{:S(2)}) collective-permute-start(f32[16,2]{0,1:T(2,128)S(1)} %get-tuple-element.757), channel_id=1, source_target_pairs={{0,4},{4,8},{8,12},{12,0},{1,5},{5,9},{9,13},{13,1},{2,6},{6,10},{... | collective-permute-start | bytes 392 | tf_op jit(solution)/shard_map/while/body/eval_jaxpr/ppermute | solution.py:14
  15.1 8.4 %collective-permute-start.1 = (f32[16,408]{0,1:T(8,128)S(1)}, f32[16,408]{0,1:T(8,128)S(1)}, u32[]{:S(2)}, u32[]{:S(2)}) collective-permute-start(f32[16,408]{0,1:T(8,128)S(1)} %get-tuple-element.756), channel_id=1, source_target_pairs={{0,4},{4,8},{8,12},{12,0},{1,5},{5,9},{9,13},{13,1},{2,6},{6,10},{... | collective-permute-start | bytes 78344 | tf_op jit(solution)/shard_map/while/body/eval_jaxpr/ppermute | solution.py:14
  23.6 0.7 copy-start.1
  25.0 0.9 %slice-start = ((f32[16,6,12,3]{0,3,2,1:T(4,128)}), f32[16,6,8,3]{0,3,2,1:T(4,128)S(1)}, s32[]{:S(2)}) async-start(f32[16,6,12,3]{0,3,2,1:T(4,128)} %copy-done.1), calls=%async_computation | async-start | bytes 196608 | tf_op jit(solution)/shard_map/while/body/eval_jaxpr/slice | solution.py:182
  26.4 5.4 %collective-permute-start = (f32[16,2]{0,1:T(2,128)S(1)}, f32[16,2]{0,1:T(2,128)S(1)}, u32[]{:S(2)}, u32[]{:S(2)}) collective-permute-start(f32[16,2]{0,1:T(2,128)S(1)} %get-tuple-element.757), channel_id=1, source_target_pairs={{0,4},{4,8},{8,12},{12,0},{1,5},{5,9},{9,13},{13,1},{2,6},{6,10},{... | collective-permute-start | bytes 392 | tf_op jit(solution)/shard_map/while/body/eval_jaxpr/ppermute | solution.py:14
  26.5 7.7 %collective-permute-start.1 = (f32[16,408]{0,1:T(8,128)S(1)}, f32[16,408]{0,1:T(8,128)S(1)}, u32[]{:S(2)}, u32[]{:S(2)}) collective-permute-start(f32[16,408]{0,1:T(8,128)S(1)} %get-tuple-element.756), channel_id=1, source_target_pairs={{0,4},{4,8},{8,12},{12,0},{1,5},{5,9},{9,13},{13,1},{2,6},{6,10},{... | collective-permute-start | bytes 78344 | tf_op jit(solution)/shard_map/while/body/eval_jaxpr/ppermute | solution.py:14
  34.2 0.7 copy-start.1
  35.6 0.9 %slice-start = ((f32[16,6,12,3]{0,3,2,1:T(4,128)}), f32[16,6,8,3]{0,3,2,1:T(4,128)S(1)}, s32[]{:S(2)}) async-start(f32[16,6,12,3]{0,3,2,1:T(4,128)} %copy-done.1), calls=%async_computation | async-start | bytes 196608 | tf_op jit(solution)/shard_map/while/body/eval_jaxpr/slice | solution.py:182
  37.0 5.4 %collective-permute-start = (f32[16,2]{0,1:T(2,128)S(1)}, f32[16,2]{0,1:T(2,128)S(1)}, u32[]{:S(2)}, u32[]{:S(2)}) collective-permute-start(f32[16,2]{0,1:T(2,128)S(1)} %get-tuple-element.757), channel_id=1, source_target_pairs={{0,4},{4,8},{8,12},{12,0},{1,5},{5,9},{9,13},{13,1},{2,6},{6,10},{... | collective-permute-start | bytes 392 | tf_op jit(solution)/shard_map/while/body/eval_jaxpr/ppermute | solution.py:14
  37.1 7.7 %collective-permute-start.1 = (f32[16,408]{0,1:T(8,128)S(1)}, f32[16,408]{0,1:T(8,128)S(1)}, u32[]{:S(2)}, u32[]{:S(2)}) collective-permute-start(f32[16,408]{0,1:T(8,128)S(1)} %get-tuple-element.756), channel_id=1, source_target_pairs={{0,4},{4,8},{8,12},{12,0},{1,5},{5,9},{9,13},{13,1},{2,6},{6,10},{... | collective-permute-start | bytes 78344 | tf_op jit(solution)/shard_map/while/body/eval_jaxpr/ppermute | solution.py:14
  44.8 0.7 copy-start.1
  46.1 0.9 %slice-start = ((f32[16,6,12,3]{0,3,2,1:T(4,128)}), f32[16,6,8,3]{0,3,2,1:T(4,128)S(1)}, s32[]{:S(2)}) async-start(f32[16,6,12,3]{0,3,2,1:T(4,128)} %copy-done.1), calls=%async_computation | async-start | bytes 196608 | tf_op jit(solution)/shard_map/while/body/eval_jaxpr/slice | solution.py:182
  60.3 9.3 %copy-start.12 = (f32[384]{0:T(512)S(1)}, f32[384]{0:T(512)}, u32[]{:S(2)}) copy-start(f32[384]{0:T(512)} %param.30) | copy-start | bytes 4612
  69.6 0.7 copy-start.11
  70.3 0.6 copy-start.5
where the time goes:
time: 86 us; the launch traced here: 85.5 us
  blocking collectives  31.6 us (37%)
  waiting for transfers between devices  18.2 us (21%)
  local copies, waits for them, and re-layouts  15 us (17%)
  matrix products  9.58 us (11%)
  starting transfers between devices  6.74 us (8%)
  other arithmetic  2.83 us (3%)
  between operations  1.1 us (1%)
    ppermute x6, waiting for transfers between devices, shifted(): lax.ppermute(array, axis, [(i, (i + by) % peers) for i in range(peers)])  18.2 us
    all_gather x1, blocking collectives, body(): frames_out = lax.all_gather(frames_new, 'blk', axis=1, tiled=True)  13.1 us
    all_gather x5, blocking collectives, combined_all(): pieces = jax.tree.map(lambda part: lax.all_gather(part, axis), value)  9.88 us
    psum x1, blocking collectives, body(): update = lax.psum(partial_update, 'head')  8.59 us
    ppermute x6, starting transfers between devices, shifted(): lax.ppermute(array, axis, [(i, (i + by) % peers) for i in range(peers)])  6.74 us
    unnamed x32, local copies, waits for them, and re-layouts  6.07 us
    while x15, local copies, waits for them, and re-layouts  1.94 us
    slice x7, local copies, waits for them, and re-layouts, absorb(): points[:, :, query_count:]  1.86 us
  transfers between devices with their start and end apart: 6, of which 6 were waited for; matrix products, arithmetic and copies ran while one was open for 2% of the time, Pallas kernels for 0%

commit v1 on v0

--- a/solution.py
+++ b/solution.py
@@ -220,7 +220,7 @@
         w_out.reshape(-1, w_out.shape[2]),
         preferred_element_type=jnp.float32,
     )
-    update = lax.psum(partial_update, "head")
+    update = jnp.sum(lax.all_gather(partial_update, "head"), axis=0)
     mixed = single.astype(jnp.float32) + update
     centre = jnp.mean(mixed, axis=1, keepdims=True)
     spread = jnp.mean(jnp.square(mixed - centre), axis=1, keepdims=True)

time: 86 us -> 82.2 us (0.956)
  blocking collectives: 31.6 us -> 27.8 us
    psum x1 -> x0, blocking collectives: 8.59 us -> none  [body(): update = lax.psum(partial_update, 'head')]
    all_gather x0 -> x1, blocking collectives: none -> 4.76 us  [body(): update = jnp.sum(lax.all_gather(partial_update, 'head'), axis=0)]
where the time goes in v1:
time: 82.2 us; the launch traced here: 81.6 us
  blocking collectives  27.8 us (34%)
  waiting for transfers between devices  18.2 us (22%)
  local copies, waits for them, and re-layouts  15 us (18%)
  matrix products  9.58 us (12%)
  starting transfers between devices  6.74 us (8%)
  other arithmetic  2.83 us (3%)
  between operations  1.1 us (1%)
    ppermute x6, waiting for transfers between devices, shifted(): lax.ppermute(array, axis, [(i, (i + by) % peers) for i in range(peers)])  18.2 us
    all_gather x1, blocking collectives, body(): frames_out = lax.all_gather(frames_new, 'blk', axis=1, tiled=True)  13.1 us
    all_gather x5, blocking collectives, combined_all(): pieces = jax.tree.map(lambda part: lax.all_gather(part, axis), value)  9.88 us
    ppermute x6, starting transfers between devices, shifted(): lax.ppermute(array, axis, [(i, (i + by) % peers) for i in range(peers)])  6.74 us
    unnamed x32, local copies, waits for them, and re-layouts  6.07 us
    all_gather x1, blocking collectives, body(): update = jnp.sum(lax.all_gather(partial_update, 'head'), axis=0)  4.76 us
    while x15, local copies, waits for them, and re-layouts  1.94 us
    slice x7, local copies, waits for them, and re-layouts, absorb(): points[:, :, query_count:]  1.86 us
  transfers between devices with their start and end apart: 6, of which 6 were waited for; matrix products, arithmetic and copies ran while one was open for 2% of the time, Pallas kernels for 0%

profile of v1, /device:TPU:0, one launch (start us, length us, event | category | flops | bytes accessed | tf_op | source)
XLA Modules:
  0.0 81.6 jit_solution(10550850342880133612)
XLA Ops:
  0.7 0.7 copy-done.13
  1.7 0.3 copy-done.8
  2.6 0.6 copy-done.3
  3.1 1.1 %fusion.59 = f32[16,192]{1,0:T(8,128)S(1)} fusion(bf16[384,192]{0,1:T(8,128)(2,1)} %param.23, bf16[32,384]{1,0:T(8,128)(2,1)S(1)} %copy-done.3, s32[]{:T(128)S(6)} %select_n.43), kind=kOutput, calls=%fused_computation.96 | convolution fusion | flops 2359296 | bytes 172036 | tf_op jit(solution)/shard_map/dot_general | solution.py:145
  4.6 0.8 copy-done.7
  5.7 0.3 convolution_add_fusion.2
  6.6 0.7 copy-done.4
  7.7 0.3 convolution_add_fusion.3
  8.4 0.3 copy-done.2
  8.7 0.3 copy-done.6
  9.0 0.4 fusion.35
  9.6 0.2 copy.240
  9.8 0.2 multiply_reduce_fusion.1
  10.1 0.4 copy-done.10
  10.5 0.2 fusion.84
  11.6 0.4 fusion.20
  12.0 35.5 %while.7 = (s32[]{:T(128)}, f32[32,6]{0,1:T(8,128)S(1)}, f32[32,6]{0,1:T(8,128)S(1)}, f32[32,6,16]{0,2,1:T(8,128)S(1)}, f32[32,6,8,3]{0,2,3,1:T(8,128)S(1)}, /*i...) while((s32[]{:T(128)}, f32[32,6]{0,1:T(8,128)S(1)}, ...), condition=%wide.region_7.8_spmd, body=%wide.region_3.7_spmd.sunk | while | flops 3855250 | bytes 1648512 | solution.py:209
  12.0 3.1 %collective-permute-start = (f32[16,2]{0,1:T(2,128)S(1)}, f32[16,2]{0,1:T(2,128)S(1)}, u32[]{:S(2)}, u32[]{:S(2)}) collective-permute-start(f32[16,2]{0,1:T(2,128)S(1)} %get-tuple-element.757), channel_id=1, source_target_pairs={{0,4},{4,8},{8,12},{12,0},{1,5},{5,9},{9,13},{13,1},{2,6},{6,10},{... | collective-permute-start | bytes 392 | tf_op jit(solution)/shard_map/while/body/eval_jaxpr/ppermute | solution.py:14
  15.1 1.6 %collective-permute-start.1 = (f32[16,408]{0,1:T(8,128)S(1)}, f32[16,408]{0,1:T(8,128)S(1)}, u32[]{:S(2)}, u32[]{:S(2)}) collective-permute-start(f32[16,408]{0,1:T(8,128)S(1)} %get-tuple-element.756), channel_id=1, source_target_pairs={{0,4},{4,8},{8,12},{12,0},{1,5},{5,9},{9,13},{13,1},{2,6},{6,10},{... | collective-permute-start | bytes 78344 | tf_op jit(solution)/shard_map/while/body/eval_jaxpr/ppermute | solution.py:14
  16.7 0.4 fusion.127
  17.2 1.5 %collective-permute-done = f32[16,2]{0,1:T(2,128)S(1)} collective-permute-done((f32[16,2]{0,1:T(2,128)S(1)}, f32[16,2]{0,1:T(2,128)S(1)}, u32[]{:S(2)}, u32[]{:S(2)}) %collective-permute-start) | collective-permute-done | bytes 160 | tf_op jit(solution)/shard_map/while/body/eval_jaxpr/ppermute | solution.py:14
  18.9 4.7 %collective-permute-done.1 = f32[16,408]{0,1:T(8,128)S(1)} collective-permute-done((f32[16,408]{0,1:T(8,128)S(1)}, f32[16,408]{0,1:T(8,128)S(1)}, u32[]{:S(2)}, u32[]{:S(2)}) %collective-permute-start.1) | collective-permute-done | bytes 26144 | tf_op jit(solution)/shard_map/while/body/eval_jaxpr/ppermute | solution.py:14
  23.7 0.6 copy-done.1
  24.3 0.2 multiply_reduce_fusion.6
  24.5 0.3 fusion.128
  25.3 0.6 slice-done
  25.9 0.3 fusion.131
  26.2 0.2 convolution_add_fusion.5
  26.5 1.4 %collective-permute-start.1 = (f32[16,408]{0,1:T(8,128)S(1)}, f32[16,408]{0,1:T(8,128)S(1)}, u32[]{:S(2)}, u32[]{:S(2)}) collective-permute-start(f32[16,408]{0,1:T(8,128)S(1)} %get-tuple-element.756), channel_id=1, source_target_pairs={{0,4},{4,8},{8,12},{12,0},{1,5},{5,9},{9,13},{13,1},{2,6},{6,10},{... | collective-permute-start | bytes 78344 | tf_op jit(solution)/shard_map/while/body/eval_jaxpr/ppermute | solution.py:14
  27.8 0.4 fusion.127
  28.3 3.5 %collective-permute-done = f32[16,2]{0,1:T(2,128)S(1)} collective-permute-done((f32[16,2]{0,1:T(2,128)S(1)}, f32[16,2]{0,1:T(2,128)S(1)}, u32[]{:S(2)}, u32[]{:S(2)}) %collective-permute-start) | collective-permute-done | bytes 160 | tf_op jit(solution)/shard_map/while/body/eval_jaxpr/ppermute | solution.py:14
  32.0 2.1 %collective-permute-done.1 = f32[16,408]{0,1:T(8,128)S(1)} collective-permute-done((f32[16,408]{0,1:T(8,128)S(1)}, f32[16,408]{0,1:T(8,128)S(1)}, u32[]{:S(2)}, u32[]{:S(2)}) %collective-permute-start.1) | collective-permute-done | bytes 26144 | tf_op jit(solution)/shard_map/while/body/eval_jaxpr/ppermute | solution.py:14
  34.2 0.6 copy-done.1
  34.9 0.2 multiply_reduce_fusion.6
  35.1 0.3 fusion.128
  35.9 0.6 slice-done
  36.4 0.3 fusion.131
  36.7 0.2 convolution_add_fusion.5
  37.1 0.6 collective-permute-start.1
  37.7 0.4 fusion.127
  38.2 4.3 %collective-permute-done = f32[16,2]{0,1:T(2,128)S(1)} collective-permute-done((f32[16,2]{0,1:T(2,128)S(1)}, f32[16,2]{0,1:T(2,128)S(1)}, u32[]{:S(2)}, u32[]{:S(2)}) %collective-permute-start) | collective-permute-done | bytes 160 | tf_op jit(solution)/shard_map/while/body/eval_jaxpr/ppermute | solution.py:14
  42.6 2.1 %collective-permute-done.1 = f32[16,408]{0,1:T(8,128)S(1)} collective-permute-done((f32[16,408]{0,1:T(8,128)S(1)}, f32[16,408]{0,1:T(8,128)S(1)}, u32[]{:S(2)}, u32[]{:S(2)}) %collective-permute-start.1) | collective-permute-done | bytes 26144 | tf_op jit(solution)/shard_map/while/body/eval_jaxpr/ppermute | solution.py:14
  44.8 0.6 copy-done.1
  45.4 0.2 multiply_reduce_fusion.6
  45.7 0.3 fusion.128
  46.4 0.6 slice-done
  47.0 0.3 fusion.131
  47.3 0.2 convolution_add_fusion.5
  47.6 1.8 %all-gather.6 = f32[2,32,6]{1,2,0:T(8,128)S(1)} all-gather(f32[1,32,6]{1,2,0:T(8,128)S(1)} %bitcast.282), channel_id=3, replica_groups=mesh['groups'=2,'blk'=4,'head'=2,'pair'=2] {'pair'}, dimensions={0}, use_global_device_ids=true | all-gather | bytes 2304 | tf_op jit(solution)/shard_map/all_gather | solution.py:18
  49.4 1.8 %all-gather.7 = f32[2,32,6]{1,2,0:T(8,128)S(1)} all-gather(f32[1,32,6]{1,2,0:T(8,128)S(1)} %bitcast.284), channel_id=4, replica_groups=mesh['groups'=2,'blk'=4,'head'=2,'pair'=2] {'pair'}, dimensions={0}, use_global_device_ids=true | all-gather | bytes 2304 | tf_op jit(solution)/shard_map/all_gather | solution.py:18
  51.5 1.9 %all-gather.4 = f32[64,6,128]{2,0,1:T(8,128)S(1)} all-gather(f32[32,6,128]{2,0,1:T(8,128)S(1)} %copy.259), channel_id=6, replica_groups=mesh['groups'=2,'blk'=4,'head'=2,'pair'=2] {'pair'}, dimensions={0}, use_global_device_ids=true | all-gather | bytes 294912 | tf_op jit(solution)/shard_map/all_gather | solution.py:18
  53.7 1.9 %all-gather = f32[64,6,16]{2,0,1:T(8,128)S(1)} all-gather(f32[32,6,16]{2,0,1:T(8,128)S(1)} %copy.249), channel_id=2, replica_groups=mesh['groups'=2,'blk'=4,'head'=2,'pair'=2] {'pair'}, dimensions={0}, use_global_device_ids=true | all-gather | bytes 36864 | tf_op jit(solution)/shard_map/all_gather | solution.py:18
  55.8 0.2 copy.250
  56.0 2.4 %all-gather.3 = f32[64,6,8,3]{2,1,3,0:T(8,128)S(1)} all-gather(f32[32,6,8,3]{2,1,3,0:T(8,128)S(1)} %copy.250), channel_id=5, replica_groups=mesh['groups'=2,'blk'=4,'head'=2,'pair'=2] {'pair'}, dimensions={0}, use_global_device_ids=true | all-gather | bytes 55296 | tf_op jit(solution)/shard_map/all_gather | solution.py:18
  58.4 0.3 fusion.30
  58.6 1.1 %fusion.82 = (bf16[32,6,8,3]{2,3,1,0:T(4,128)(2,1)S(1)}, f32[32,6,8]{2,1,0:T(8,128)S(1)}) fusion(f32[3,3,32,1]{0,1,3,2:T(4,128)S(1)} %copy.271, f32[32,6,8,3]{2,1,3,0:T(8,128)S(1)} %fusion.30), kind=kOutput, calls=%fused_computation.152 | convolution fusion | flops 178176 | bytes 34944 | tf_op jit(solution)/shard_map/abn,nhpa->nhpb/dot_general | solution.py:34
  59.7 0.2 copy.257
  60.3 0.4 convolution_bitcast_fusion.4
  60.7 4.8 %all-gather.5 = f32[64,384]{1,0:T(8,128)S(1)} all-gather(f32[32,384]{1,0:T(8,128)S(1)} %convolution_bitcast_fusion.4), channel_id=7, replica_groups=mesh['groups'=2,'blk'=4,'head'=2,'pair'=2] {'head'}, dimensions={0}, use_global_device_ids=true | all-gather | bytes 147456 | tf_op jit(solution)/shard_map/all_gather | solution.py:223
  65.9 0.6 copy-done.11
  66.6 0.4 copy-done.5
  67.3 0.3 convolution_bitcast_fusion.3
  67.8 13.1 %all-gather.8 = f32[4,32,12]{1,2,0:T(8,128)S(1)} all-gather(f32[1,32,12]{1,2,0:T(8,128)S(1)} %maximum_bitcast_fusion), channel_id=1, replica_groups=mesh['groups'=2,'blk'=4,'head'=2,'pair'=2] {'blk'}, dimensions={0}, use_global_device_ids=true | all-gather | bytes 7680 | tf_op jit(solution)/shard_map/all_gather | solution.py:230
  80.9 0.7 reshape.715
  (161 shorter events, 8.1 us)
Async XLA Ops:
  0.6 59.6 %copy-start = (bf16[6,176,384]{2,1,0:T(8,128)(2,1)S(1)}, bf16[6,176,384]{2,1,0:T(8,128)(2,1)}, u32[]{:S(2)}) copy-start(bf16[6,176,384]{2,1,0:T(8,128)(2,1)} %param.29) | copy-start | bytes 2433028
  0.7 0.7 copy-start.13
  0.7 0.7 copy-start.14
  0.7 0.7 copy-start.15
  1.4 0.7 copy-start.8
  2.4 0.7 copy-start.3
  3.1 1.2 %copy-start.9 = (bf16[384,72]{0,1:T(8,128)(2,1)S(1)}, bf16[384,72]{0,1:T(8,128)(2,1)}, u32[]{:S(2)}) copy-start(bf16[384,72]{0,1:T(8,128)(2,1)} %param.24) | copy-start | bytes 165892
  4.5 0.9 %copy-start.7 = (bf16[384,96]{0,1:T(8,128)(2,1)S(1)}, bf16[384,96]{0,1:T(8,128)(2,1)}, u32[]{:S(2)}) copy-start(bf16[384,96]{0,1:T(8,128)(2,1)} %param.22) | copy-start | bytes 221188
  6.5 0.9 %copy-start.4 = (bf16[384,216]{0,1:T(8,128)(2,1)S(1)}, bf16[384,216]{0,1:T(8,128)(2,1)}, u32[]{:S(2)}) copy-start(bf16[384,216]{0,1:T(8,128)(2,1)} %param.25) | copy-start | bytes 497668
  7.6 1.0 %copy-start.2 = (bf16[32,4,16,128]{3,2,1,0:T(8,128)(2,1)S(1)}, bf16[32,4,16,128]{3,2,1,0:T(8,128)(2,1)}, u32[]{:S(2)}) copy-start(bf16[32,4,16,128]{3,2,1,0:T(8,128)(2,1)} %param.18) | copy-start | bytes 1572868
  8.3 0.7 copy-start.6
  9.8 0.7 copy-start.10
  12.0 6.7 %collective-permute-start = (f32[16,2]{0,1:T(2,128)S(1)}, f32[16,2]{0,1:T(2,128)S(1)}, u32[]{:S(2)}, u32[]{:S(2)}) collective-permute-start(f32[16,2]{0,1:T(2,128)S(1)} %get-tuple-element.757), channel_id=1, source_target_pairs={{0,4},{4,8},{8,12},{12,0},{1,5},{5,9},{9,13},{13,1},{2,6},{6,10},{... | collective-permute-start | bytes 392 | tf_op jit(solution)/shard_map/while/body/eval_jaxpr/ppermute | solution.py:14
  15.1 8.4 %collective-permute-start.1 = (f32[16,408]{0,1:T(8,128)S(1)}, f32[16,408]{0,1:T(8,128)S(1)}, u32[]{:S(2)}, u32[]{:S(2)}) collective-permute-start(f32[16,408]{0,1:T(8,128)S(1)} %get-tuple-element.756), channel_id=1, source_target_pairs={{0,4},{4,8},{8,12},{12,0},{1,5},{5,9},{9,13},{13,1},{2,6},{6,10},{... | collective-permute-start | bytes 78344 | tf_op jit(solution)/shard_map/while/body/eval_jaxpr/ppermute | solution.py:14
  23.6 0.7 copy-start.1
  25.0 0.9 %slice-start = ((f32[16,6,12,3]{0,3,2,1:T(4,128)}), f32[16,6,8,3]{0,3,2,1:T(4,128)S(1)}, s32[]{:S(2)}) async-start(f32[16,6,12,3]{0,3,2,1:T(4,128)} %copy-done.1), calls=%async_computation | async-start | bytes 196608 | tf_op jit(solution)/shard_map/while/body/eval_jaxpr/slice | solution.py:182
  26.4 5.4 %collective-permute-start = (f32[16,2]{0,1:T(2,128)S(1)}, f32[16,2]{0,1:T(2,128)S(1)}, u32[]{:S(2)}, u32[]{:S(2)}) collective-permute-start(f32[16,2]{0,1:T(2,128)S(1)} %get-tuple-element.757), channel_id=1, source_target_pairs={{0,4},{4,8},{8,12},{12,0},{1,5},{5,9},{9,13},{13,1},{2,6},{6,10},{... | collective-permute-start | bytes 392 | tf_op jit(solution)/shard_map/while/body/eval_jaxpr/ppermute | solution.py:14
  26.5 7.7 %collective-permute-start.1 = (f32[16,408]{0,1:T(8,128)S(1)}, f32[16,408]{0,1:T(8,128)S(1)}, u32[]{:S(2)}, u32[]{:S(2)}) collective-permute-start(f32[16,408]{0,1:T(8,128)S(1)} %get-tuple-element.756), channel_id=1, source_target_pairs={{0,4},{4,8},{8,12},{12,0},{1,5},{5,9},{9,13},{13,1},{2,6},{6,10},{... | collective-permute-start | bytes 78344 | tf_op jit(solution)/shard_map/while/body/eval_jaxpr/ppermute | solution.py:14
  34.2 0.7 copy-start.1
  35.6 0.9 %slice-start = ((f32[16,6,12,3]{0,3,2,1:T(4,128)}), f32[16,6,8,3]{0,3,2,1:T(4,128)S(1)}, s32[]{:S(2)}) async-start(f32[16,6,12,3]{0,3,2,1:T(4,128)} %copy-done.1), calls=%async_computation | async-start | bytes 196608 | tf_op jit(solution)/shard_map/while/body/eval_jaxpr/slice | solution.py:182
  37.0 5.4 %collective-permute-start = (f32[16,2]{0,1:T(2,128)S(1)}, f32[16,2]{0,1:T(2,128)S(1)}, u32[]{:S(2)}, u32[]{:S(2)}) collective-permute-start(f32[16,2]{0,1:T(2,128)S(1)} %get-tuple-element.757), channel_id=1, source_target_pairs={{0,4},{4,8},{8,12},{12,0},{1,5},{5,9},{9,13},{13,1},{2,6},{6,10},{... | collective-permute-start | bytes 392 | tf_op jit(solution)/shard_map/while/body/eval_jaxpr/ppermute | solution.py:14
  37.1 7.7 %collective-permute-start.1 = (f32[16,408]{0,1:T(8,128)S(1)}, f32[16,408]{0,1:T(8,128)S(1)}, u32[]{:S(2)}, u32[]{:S(2)}) collective-permute-start(f32[16,408]{0,1:T(8,128)S(1)} %get-tuple-element.756), channel_id=1, source_target_pairs={{0,4},{4,8},{8,12},{12,0},{1,5},{5,9},{9,13},{13,1},{2,6},{6,10},{... | collective-permute-start | bytes 78344 | tf_op jit(solution)/shard_map/while/body/eval_jaxpr/ppermute | solution.py:14
  44.8 0.7 copy-start.1
  46.1 0.9 %slice-start = ((f32[16,6,12,3]{0,3,2,1:T(4,128)}), f32[16,6,8,3]{0,3,2,1:T(4,128)S(1)}, s32[]{:S(2)}) async-start(f32[16,6,12,3]{0,3,2,1:T(4,128)} %copy-done.1), calls=%async_computation | async-start | bytes 196608 | tf_op jit(solution)/shard_map/while/body/eval_jaxpr/slice | solution.py:182
  60.7 5.1 %copy-start.12 = (f32[384]{0:T(512)S(1)}, f32[384]{0:T(512)}, u32[]{:S(2)}) copy-start(f32[384]{0:T(512)} %param.30) | copy-start | bytes 4612
  65.8 0.7 copy-start.11
  66.5 0.6 copy-start.5
